TPU v7x, 256 devices: a whole 4x4x8 slice. The times are simulated.
256 devices in a mesh: row: 8 (over y, core), col: 32 (over z, x).
Axes of the slice: x: 4, y: 4, z: 8, core: 2. Of those that a mesh axis runs over, the one named last changes fastest.
Arguments:
- embeds: bfloat16 [3072, 8192], P('row', 'col'), may hold values from -600 to 600
- ln_gain: float32 [8192], replicated, may hold values from 0.1 to 1.9
- ln_bias: float32 [8192], replicated, may hold values from -3 to 3
- w_qkv: bfloat16 [8192, 24576], P('row', 'col'), may hold values from -4 to 4, as said below
- w_out: bfloat16 [8192, 8192], P('row', 'col'), may hold values from -0.0625 to 0.0625
- out_bias: float32 [8192], P('col'), may hold values from -3 to 3
Outputs:
- attended: bfloat16 [3072, 8192], P('row', 'col')
Inputs may be any that keep to these rules, and one draw needn't show every extreme that they name: Columns of w_qkv are ordered by head, then query, key, value, then entry of the head.
All inputs are finite; a program needn't handle non-finite values.
Results may differ from a plain program's by a relative error of at most 0.0065.
Values may be sent and summed in bfloat16 or wider, within the bound.
A program may use at most 64 MiB of HBM per device.

v0:
```python
import jax
import jax.numpy as jnp
from jax import lax
from jax.sharding import PartitionSpec as P

D = 8192
HEADS = 64
SEQ = 128


def normalize(values, mean, var, gain, shift):
    return ((values - mean) * lax.rsqrt(var + 1e-05) * gain + shift).astype(jnp.bfloat16)


def attend(qkv):
    total, columns = qkv.shape
    head_size = D // HEADS
    heads = columns // (3 * head_size)
    packed = qkv.reshape(total // SEQ, SEQ, heads, 3, head_size)
    query = packed[:, :, :, 0]
    keys = packed[:, :, :, 1]
    vals = packed[:, :, :, 2]
    scores = jnp.einsum("nqhd,nkhd->nhqk", query, keys, preferred_element_type=jnp.float32)
    scores = scores / jnp.sqrt(jnp.float32(head_size))
    peak = jnp.max(scores, axis=-1, keepdims=True)
    expo = jnp.exp(scores - peak)
    probs = (expo / jnp.sum(expo, axis=-1, keepdims=True)).astype(jnp.bfloat16)
    context = jnp.einsum("nhqk,nkhd->nqhd", probs, vals, preferred_element_type=jnp.float32)
    return context.astype(jnp.bfloat16).reshape(total, heads * head_size)


def on_device(embeds, ln_gain, ln_bias, w_qkv, w_out, out_bias):
    width = embeds.shape[1]
    offset = lax.axis_index("col") * width
    values = embeds.astype(jnp.float32)
    gain_part = lax.dynamic_slice_in_dim(ln_gain, offset, width)
    bias_part = lax.dynamic_slice_in_dim(ln_bias, offset, width)
    mean = lax.psum(jnp.sum(values, axis=1), "col")[:, None] / D
    spread = lax.psum(jnp.sum((values - mean) ** 2, axis=1), "col")
    payload = normalize(values, mean, spread[:, None] / D, gain_part, bias_part)
    gathered = lax.all_gather(payload, "col", axis=1, tiled=True)
    left = gathered
    qkv = jnp.dot(
        left, lax.all_gather(w_qkv, "row", axis=0, tiled=True), preferred_element_type=jnp.float32
    )
    context = attend(qkv.astype(jnp.bfloat16))
    full_context = lax.all_gather(context, "col", axis=1, tiled=True)
    left = full_context
    result = jnp.dot(
        left, lax.all_gather(w_out, "row", axis=0, tiled=True), preferred_element_type=jnp.float32
    )
    return (result + out_bias).astype(jnp.bfloat16)


def solution(mesh):
    return jax.shard_map(
        on_device,
        mesh=mesh,
        in_specs=(P("row", "col"), P(), P(), P("row", "col"), P("row", "col"), P("col")),
        out_specs=P("row", "col"),
        check_vma=False,
    )
```

profile of v0, /device:TPU:2, one launch (start us, length us, event | category | flops | bytes accessed | tf_op | source)
XLA Modules:
  0.0 464.5 jit_solution(14634312466143647871)
XLA Ops:
  6.5 0.8 dynamic_slice.6
  7.3 0.8 dynamic_slice.7
  8.1 1.1 convert_reduce_fusion
  9.1 73.7 %psum.14 = f32[384]{0:T(512)S(1)} all-reduce(f32[384]{0:T(512)S(1)} %convert_reduce_fusion), channel_id=1, replica_groups=mesh['row'=8,'col'=32] {'col'}, use_global_device_ids=true, to_apply=%region_1.0 | all-reduce | flops 384 | bytes 3072 | tf_op jit(solution)/shard_map/psum | solution.py:38
  82.8 1.2 fusion.7
  84.0 74.1 %psum.15 = f32[384]{0:T(512)S(1)} all-reduce(f32[384]{0:T(512)S(1)} %fusion.7), channel_id=1, replica_groups=mesh['row'=8,'col'=32] {'col'}, use_global_device_ids=true, to_apply=%region_3.0 | all-reduce | flops 384 | bytes 3072 | tf_op jit(solution)/shard_map/psum | solution.py:39
  158.1 1.8 fusion.10
  159.9 0.0 all-gather.7.cloned.1.call-start
  160.0 0.7 all-gather.7.cloned.1.call-update
  160.7 0.7 all-gather.11.cloned.1.call-update
  161.4 86.2 %all-gather.5.cloned.1.call-done = bf16[384,8192]{1,0:T(8,128)(2,1)} async-done(((bf16[384,256]{1,0:T(8,128)(2,1)}), bf16[384,8192]{1,0:T(8,128)(2,1)}) %all-gather.5.cloned.1.call-update) | async-done | bytes 6291472 | tf_op jit(solution)/shard_map/all_gather | solution.py:41
  247.7 72.7 %all-gather.7.cloned.1.call-done = bf16[8192,768]{1,0:T(8,128)(2,1)} async-done(((bf16[1024,768]{1,0:T(8,128)(2,1)}), bf16[8192,768]{1,0:T(8,128)(2,1)}) %all-gather.7.cloned.1.call-update) | async-done | bytes 12582928 | tf_op jit(solution)/shard_map/all_gather | solution.py:44
  320.4 10.8 %convolution_convert_fusion = bf16[384,768]{1,0:T(8,128)(2,1)S(1)} fusion(bf16[384,8192]{1,0:T(8,128)(2,1)} %all-gather.5.cloned.1.call-done, bf16[8192,768]{1,0:T(8,128)(2,1)} %all-gather.7.cloned.1.call-done), kind=kOutput, calls=%fused_computation.1 | convolution fusion | flops 4832133120 | bytes 19464192 | tf_op jit(solution)/shard_map/dot_general | solution.py:43
  331.2 0.3 reshape.17
  331.5 0.9 fusion.15
  332.3 0.6 copy.17
  332.9 0.3 fusion.16
  333.3 0.3 convolution_multiply_fusion
  333.5 0.3 fusion.4
  333.8 0.2 copy.15
  334.0 0.7 copy.34
  334.7 22.6 %all-gather.11.cloned.1.call-done = bf16[8192,256]{1,0:T(8,128)(2,1)} async-done(((bf16[1024,256]{1,0:T(8,128)(2,1)}), bf16[8192,256]{1,0:T(8,128)(2,1)}) %all-gather.11.cloned.1.call-update) | async-done | bytes 4194320 | tf_op jit(solution)/shard_map/all_gather | solution.py:50
  357.3 94.2 %all-gather.9.cloned.1.call-done = bf16[384,8192]{1,0:T(8,128)(2,1)} async-done(((bf16[384,256]{1,0:T(8,128)(2,1)}), bf16[384,8192]{1,0:T(8,128)(2,1)}) %all-gather.9.cloned.1.call-update) | async-done | bytes 6291472 | tf_op jit(solution)/shard_map/all_gather | solution.py:47
  451.5 6.5 %fusion.3 = bf16[384,256]{1,0:T(8,128)(2,1)} fusion(bf16[384,8192]{1,0:T(8,128)(2,1)} %all-gather.9.cloned.1.call-done, bf16[8192,256]{1,0:T(8,128)(2,1)} %all-gather.11.cloned.1.call-done, f32[256]{0:T(256)S(1)} %copy-done), kind=kOutput, calls=%fused_computation.6 | convolution fusion | flops 1610809344 | bytes 10683392 | tf_op jit(solution)/shard_map/dot_general | solution.py:49
  (9 shorter events, 0.1 us)
Async XLA Ops:
  6.5 241.1 %all-gather.5.cloned.1.call-start = ((), (), s32[]{:S(2)}) async-start(), calls=%async_computation | async-start | bytes 6488064 | tf_op jit(solution)/shard_map/all_gather | solution.py:41
  159.9 160.5 %all-gather.7.cloned.1.call-start = ((), (), s32[]{:S(2)}) async-start(), calls=%async_computation.1 | async-start | bytes 14155776 | tf_op jit(solution)/shard_map/all_gather | solution.py:44
  160.7 196.6 %all-gather.11.cloned.1.call-start = ((), (), s32[]{:S(2)}) async-start(), calls=%async_computation.3 | async-start | bytes 4718592 | tf_op jit(solution)/shard_map/all_gather | solution.py:50
  161.4 290.1 %all-gather.9.cloned.1.call-start = ((), (), s32[]{:S(2)}) async-start(), calls=%async_computation.2 | async-start | bytes 6488064 | tf_op jit(solution)/shard_map/all_gather | solution.py:47
  331.2 120.3 %copy-start = (f32[256]{0:T(256)S(1)}, f32[256]{0:T(256)}, u32[]{:S(2)}) copy-start(f32[256]{0:T(256)} %param.11) | copy-start | bytes 3076
Sparse Core Ops, SparseCore 0:
  160.0 87.5 all-gather.4
  249.5 70.8 all-gather.6
  322.3 35.0 all-gather.10
  359.6 91.8 all-gather.8
where the time goes:
time: 466 us; the launch traced here: 465 us
  waiting for transfers between devices  277 us (59%)
  blocking collectives  148 us (32%)
  matrix products  18.1 us (4%)
  between operations  13.2 us (3%)
    all_gather x1, waiting for transfers between devices, on_device(): full_context = lax.all_gather(context, 'col', axis=1, tiled=True)  94.2 us
    all_gather x1, waiting for transfers between devices, on_device(): gathered = lax.all_gather(payload, 'col', axis=1, tiled=True)  86.2 us
    psum x1, blocking collectives, on_device(): spread = lax.psum(jnp.sum((values - mean) ** 2, axis=1), 'col')  74.1 us
    psum x1, blocking collectives, on_device(): mean = lax.psum(jnp.sum(values, axis=1), 'col')[:, None] / D  73.7 us
    all_gather x1, waiting for transfers between devices, on_device(): lax.all_gather(w_qkv, 'row', axis=0, tiled=True)  72.7 us
    all_gather x1, waiting for transfers between devices, on_device(): lax.all_gather(w_out, 'row', axis=0, tiled=True)  22.6 us
    dot_general x1, matrix products, on_device(): jnp.dot(left, lax.all_gather(w_qkv, 'row', axis=0, tiled=True), preferred...  10.8 us
  transfers between devices with their start and end apart: 4, of which 4 were waited for; matrix products, arithmetic and copies ran while one was open for 3% of the time, Pallas kernels for 0%

commit v1 on v0

--- a/solution.py
+++ b/solution.py
@@ -30,15 +30,10 @@
 
 
 def on_device(embeds, ln_gain, ln_bias, w_qkv, w_out, out_bias):
-    width = embeds.shape[1]
-    offset = lax.axis_index("col") * width
-    values = embeds.astype(jnp.float32)
-    gain_part = lax.dynamic_slice_in_dim(ln_gain, offset, width)
-    bias_part = lax.dynamic_slice_in_dim(ln_bias, offset, width)
-    mean = lax.psum(jnp.sum(values, axis=1), "col")[:, None] / D
-    spread = lax.psum(jnp.sum((values - mean) ** 2, axis=1), "col")
-    payload = normalize(values, mean, spread[:, None] / D, gain_part, bias_part)
-    gathered = lax.all_gather(payload, "col", axis=1, tiled=True)
+    values = lax.all_gather(embeds, "col", axis=1, tiled=True).astype(jnp.float32)
+    mean = jnp.mean(values, axis=1, keepdims=True)
+    var = jnp.mean((values - mean) ** 2, axis=1, keepdims=True)
+    gathered = normalize(values, mean, var, ln_gain, ln_bias)
     left = gathered
     qkv = jnp.dot(
         left, lax.all_gather(w_qkv, "row", axis=0, tiled=True), preferred_element_type=jnp.float32

time: 466 us -> 323 us (0.69)
  blocking collectives: 148 us -> 0 us
    psum x2 -> x0, blocking collectives: 148 us -> none  [the longest x1 74.1 us: on_device(): spread = lax.psum(jnp.sum((values - mean) ** 2, axis=1), 'col')]
    all_gather x1, waiting for transfers between devices: 86.2 us -> 95.9 us  [on_device(): lax.all_gather(embeds, 'col', axis=1, tiled=True).astype(jnp.float32)]
    all_gather x1, waiting for transfers between devices: 72.7 us -> 64.4 us  [on_device(): lax.all_gather(w_qkv, 'row', axis=0, tiled=True)]
    reduce_sum x2, other arithmetic: 2.22 us -> 8.27 us  [the longest x1 4.57 us: on_device(): var = jnp.mean((values - mean) ** 2, axis=1, keepdims=True)]
  transfers between devices with their start and end apart: 4 -> 4, of which waited for: 4 -> 4; matrix products, arithmetic and copies ran while one was open for 3% -> 7% of each run, Pallas kernels for 0% -> 0%
where the time goes in v1:
time: 323 us; the launch traced here: 322 us
  waiting for transfers between devices  278 us (86%)
  matrix products  18.9 us (6%)
  between operations  13.2 us (4%)
  other arithmetic  8.28 us (3%)
    all_gather x1, waiting for transfers between devices, on_device(): lax.all_gather(embeds, 'col', axis=1, tiled=True).astype(jnp.float32)  95.9 us
    all_gather x1, waiting for transfers between devices, on_device(): full_context = lax.all_gather(context, 'col', axis=1, tiled=True)  94.2 us
    all_gather x1, waiting for transfers between devices, on_device(): lax.all_gather(w_qkv, 'row', axis=0, tiled=True)  64.4 us
    all_gather x1, waiting for transfers between devices, on_device(): lax.all_gather(w_out, 'row', axis=0, tiled=True)  21.8 us
    dot_general x1, matrix products, on_device(): jnp.dot(left, lax.all_gather(w_qkv, 'row', axis=0, tiled=True), preferred...  11.6 us
    dot_general x1, matrix products, on_device(): jnp.dot(left, lax.all_gather(w_out, 'row', axis=0, tiled=True), preferred...  6.47 us
  transfers between devices with their start and end apart: 4, of which 4 were waited for; matrix products, arithmetic and copies ran while one was open for 7% of the time, Pallas kernels for 0%

profile of v1, /device:TPU:2, one launch (start us, length us, event | category | flops | bytes accessed | tf_op | source)
XLA Modules:
  0.0 321.5 jit_solution(9538587884315066890)
XLA Ops:
  6.5 0.7 all-gather.5.cloned.1.call-update
  7.3 0.0 all-gather.7.cloned.1.call-start
  7.3 0.7 all-gather.7.cloned.1.call-update
  8.0 0.0 all-gather.11.cloned.1.call-start
  8.1 0.7 all-gather.11.cloned.1.call-update
  8.7 0.0 all-gather.9.cloned.1.call-start
  8.8 95.9 %all-gather.5.cloned.1.call-done = bf16[384,8192]{1,0:T(8,128)(2,1)} async-done(((bf16[384,256]{1,0:T(8,128)(2,1)}), bf16[384,8192]{1,0:T(8,128)(2,1)}) %all-gather.5.cloned.1.call-update) | async-done | bytes 6291472 | tf_op jit(solution)/shard_map/all_gather | solution.py:33
  104.7 3.7 %convert_reduce_fusion = f32[384]{0:T(512)S(1)} fusion(bf16[384,8192]{1,0:T(8,128)(2,1)} %all-gather.5.cloned.1.call-done), kind=kLoop, calls=%fused_computation.2 | loop fusion | flops 6291072 | bytes 6292992 | tf_op jit(solution)/shard_map/reduce_sum | solution.py:34
  108.4 4.6 %fusion.3 = f32[384]{0:T(512)S(1)} fusion(bf16[384,8192]{1,0:T(8,128)(2,1)} %all-gather.5.cloned.1.call-done, f32[384]{0:T(512)S(1)} %broadcast_multiply_fusion), kind=kLoop, calls=%fused_computation.5 | loop fusion | flops 12582528 | bytes 6294528 | tf_op jit(solution)/shard_map/reduce_sum | solution.py:35
  112.9 0.0 copy-start.2
  113.0 64.4 %all-gather.7.cloned.1.call-done = bf16[8192,768]{1,0:T(8,128)(2,1)} async-done(((bf16[1024,768]{1,0:T(8,128)(2,1)}), bf16[8192,768]{1,0:T(8,128)(2,1)}) %all-gather.7.cloned.1.call-update) | async-done | bytes 12582928 | tf_op jit(solution)/shard_map/all_gather | solution.py:39
  177.4 11.6 %fusion.13 = bf16[384,768]{1,0:T(8,128)(2,1)S(1)} fusion(bf16[8192,768]{1,0:T(8,128)(2,1)} %all-gather.7.cloned.1.call-done, bf16[384,8192]{1,0:T(8,128)(2,1)} %all-gather.5.cloned.1.call-done, f32[8192]{0:T(1024)S(1)} %copy-done, f32[8192]{0:T(1024)S(1)} %copy-done.1, f32[384]{0:T(512)S(1)} %add_rsqrt_fusion, f32[384]{0:T(512)S(1)} %broadcast_multiply_fusion), kind=kOutput, calls=%fused_computation.14 | convolution fusion | flops 4851007488 | bytes 19532800 | tf_op jit(solution)/shard_map/dot_general | solution.py:38
  189.0 0.3 reshape.23
  189.3 0.9 fusion.24
  190.1 0.6 copy.17
  190.7 0.3 fusion.25
  191.0 0.3 convolution_multiply_fusion
  191.3 0.3 fusion.19
  191.6 0.2 copy.15
  191.7 0.7 copy.34
  192.5 0.0 all-gather.9.cloned.1.call-update
  192.5 21.8 %all-gather.11.cloned.1.call-done = bf16[8192,256]{1,0:T(8,128)(2,1)} async-done(((bf16[1024,256]{1,0:T(8,128)(2,1)}), bf16[8192,256]{1,0:T(8,128)(2,1)}) %all-gather.11.cloned.1.call-update) | async-done | bytes 4194320 | tf_op jit(solution)/shard_map/all_gather | solution.py:45
  214.3 94.2 %all-gather.9.cloned.1.call-done = bf16[384,8192]{1,0:T(8,128)(2,1)} async-done(((bf16[384,256]{1,0:T(8,128)(2,1)}), bf16[384,8192]{1,0:T(8,128)(2,1)}) %all-gather.9.cloned.1.call-update) | async-done | bytes 6291472 | tf_op jit(solution)/shard_map/all_gather | solution.py:42
  308.5 6.5 %fusion.18 = bf16[384,256]{1,0:T(8,128)(2,1)} fusion(bf16[384,8192]{1,0:T(8,128)(2,1)} %all-gather.9.cloned.1.call-done, bf16[8192,256]{1,0:T(8,128)(2,1)} %all-gather.11.cloned.1.call-done, f32[256]{0:T(256)S(1)} %copy-done.2), kind=kOutput, calls=%fused_computation.19 | convolution fusion | flops 1610809344 | bytes 10683392 | tf_op jit(solution)/shard_map/dot_general | solution.py:44
  (8 shorter events, 0.0 us)
Async XLA Ops:
  6.5 170.9 %copy-start.1 = (f32[8192]{0:T(1024)S(1)}, f32[8192]{0:T(1024)}, u32[]{:S(2)}) copy-start(f32[8192]{0:T(1024)} %param.7) | copy-start | bytes 98308
  6.5 170.9 %copy-start = (f32[8192]{0:T(1024)S(1)}, f32[8192]{0:T(1024)}, u32[]{:S(2)}) copy-start(f32[8192]{0:T(1024)} %param.8) | copy-start | bytes 98308
  6.5 98.1 %all-gather.5.cloned.1.call-start = ((), (), s32[]{:S(2)}) async-start(), calls=%async_computation | async-start | bytes 6488064 | tf_op jit(solution)/shard_map/all_gather | solution.py:33
  7.3 170.1 %all-gather.7.cloned.1.call-start = ((), (), s32[]{:S(2)}) async-start(), calls=%async_computation.1 | async-start | bytes 14155776 | tf_op jit(solution)/shard_map/all_gather | solution.py:39
  8.0 206.3 %all-gather.11.cloned.1.call-start = ((), (), s32[]{:S(2)}) async-start(), calls=%async_computation.3 | async-start | bytes 4718592 | tf_op jit(solution)/shard_map/all_gather | solution.py:45
  8.7 299.8 %all-gather.9.cloned.1.call-start = ((), (), s32[]{:S(2)}) async-start(), calls=%async_computation.2 | async-start | bytes 6488064 | tf_op jit(solution)/shard_map/all_gather | solution.py:42
  112.9 195.6 %copy-start.2 = (f32[256]{0:T(256)S(1)}, f32[256]{0:T(256)}, u32[]{:S(2)}) copy-start(f32[256]{0:T(256)} %param.11) | copy-start | bytes 3076
Sparse Core Ops, SparseCore 0:
  9.8 94.8 all-gather.4
  106.5 70.8 all-gather.6
  179.3 35.0 all-gather.10
  216.6 91.8 all-gather.8

commit v2 on v1

v2 whole, which is shorter than its diff:
```python
import functools
import heapq

import jax
import jax.numpy as jnp
from jax import lax
from jax.experimental import pallas as pl
from jax.experimental.pallas import tpu as pltpu
from jax.sharding import PartitionSpec as P

D = 8192
SEQ = 128
HEAD = 128
TOK = 384
WIDTH = 256
NX, NY, NZ = 4, 4, 8
CUT = 160
WQ = 4
QROWS = 1024 // WQ
MESH = pl.DeviceIdType.MESH


class Plan:
    def __init__(self):
        self.copies = {}
        self.steps = {}

    def copy(self, name, link, size, src, dst, landed, needs=(), level=0):
        self.copies[name] = dict(
            name=name, link=link, size=size, src=src, dst=dst, landed=landed, needs=tuple(needs), level=level,
            index=len(self.copies),
        )

    def step(self, name, cost, run, needs=(), level=0):
        self.steps[name] = dict(name=name, cost=cost, run=run, needs=tuple(needs), level=level)

    def order(self, rate, lag):
        now, when, free = 0.0, {}, {}
        waiting = {**self.copies, **self.steps}
        result = []
        while waiting:
            best = None
            for name, item in waiting.items():
                times = [when.get(need) for need in item["needs"]]
                if any(t is None for t in times):
                    continue
                ready = max(times, default=0.0)
                key = (max(ready, now), item["level"], ready, name in self.steps)
                if best is None or key < best[0]:
                    best = (key, name)
            key, name = best
            item = waiting.pop(name)
            now = key[0]
            result.append(name)
            if name in self.steps:
                now += item["cost"]
                when[name] = now
            else:
                now += 0.03
                link = item["link"]
                begin = max(now, free.get(link, 0.0))
                free[link] = begin + item["size"] / rate[link[0]]
                when[name] = free[link] + lag[link[0]]
        self.when = when
        return result


def ring(plan, axis, n, tag, block, rows, size, needs, level):
    low, high = rows
    middle = (low + high) // 2
    done = {0: list(needs)}
    for sign, mark in ((-1, "p"), (1, "m")):
        previous = list(needs)
        for hop in range(1, n // 2 + 1):
            half = hop == n // 2
            part = ((low, middle) if mark == "p" else (middle, high)) if half else rows
            name = f"{tag}.{axis}{mark}{hop}"
            plan.copy(
                name, axis + mark, size * (part[1] - part[0]),
                block(sign * (hop - 1), part), block(sign * (hop - 1), part), block(sign * hop, part),
                previous, level,
            )
            previous = [name]
            done.setdefault((sign * hop) % n, []).append(name)
    return done


def gather(plan, tag, slot, size, needs, level):
    done = {offset: [] for offset in range(NZ)}
    first, second = (0, CUT), (CUT, TOK)
    across = ring(plan, "x", NX, tag + "a", lambda o, r: functools.partial(slot, 0, o, r), first, size, needs, level)
    along = ring(plan, "z", NZ, tag + "b", lambda o, r: functools.partial(slot, o, 0, r), second, size, needs, level)
    for at, arrivals in across.items():
        found = ring(
            plan, "z", NZ, f"{tag}a{at}", lambda o, r, at=at: functools.partial(slot, o, at, r), first, size, arrivals, level
        )
        for offset, names in found.items():
            done[offset] += names
    for at, arrivals in along.items():
        found = ring(
            plan, "x", NX, f"{tag}b{at}", lambda o, r, at=at: functools.partial(slot, at, o, r), second, size, arrivals, level
        )
        for names in found.values():
            done[at] += names
    return done


def to_columns(row):
    return jnp.transpose(jnp.broadcast_to(row, (128, TOK)))


def kernel(embeds, gain, shift, w_qkv, w_out, out_bias, out, normed, wide, last, ctx, total, sums, stat_x, stat_z,
           send_sem, recv_sem, own_sem):
    row, col = lax.axis_index("row"), lax.axis_index("col")
    y, core = row // 2, row % 2
    z, x = col // NX, col % NX

    def at(dx=0, dy=0, dz=0, other=0):
        their_core = 1 - core if other else core
        return (2 * ((y + dy + NY) % NY) + their_core, NX * ((z + dz + NZ) % NZ) + (x + dx + NX) % NX)

    near = dict(
        xp=at(dx=1), xm=at(dx=-1), yp=at(dy=1), ym=at(dy=-1), zp=at(dz=1), zm=at(dz=-1), c=at(other=1)
    )
    for d in range(1, NX):
        near[f"sx{d}"] = at(dx=d)
    for d in range(1, NZ):
        near[f"sz{d}"] = at(dz=d)

    plan = Plan()

    lines = lax.broadcasted_iota(jnp.int32, (8, TOK), 0)

    def pack(total_, spread):
        return jnp.where(lines == 0, total_, jnp.where(lines == 1, spread, 0.0))

    def merge(stats, n, count):
        totals = [stats[i][0:1] for i in range(n)]
        full = functools.reduce(jnp.add, totals)
        mean = full * (1.0 / (n * count))
        spread = functools.reduce(jnp.add, [stats[i][1:2] for i in range(n)])
        apart = functools.reduce(jnp.add, [(t * (1.0 / count) - mean) ** 2 for t in totals])
        return full, mean, spread + count * apart

    def stats_own():
        values = embeds[...].astype(jnp.float32)
        summed = jnp.sum(values, axis=1, keepdims=True)
        apart = values - summed * (1.0 / WIDTH)
        spread = jnp.sum(apart * apart, axis=1, keepdims=True)
        lane = lax.broadcasted_iota(jnp.int32, (TOK, 128), 1)
        both = jnp.where(lane == 0, summed, jnp.where(lane == 1, spread, 0.0))
        stat_x[x] = jnp.transpose(both)[0:8]

    def stats_x():
        full, _, spread = merge(stat_x, NX, WIDTH)
        stat_z[z] = pack(full, spread)

    def norm():
        _, mean, spread = merge(stat_z, NZ, NX * WIDTH)
        scale = lax.rsqrt(spread * (1.0 / D) + 1e-05)
        mean, scale = to_columns(mean), to_columns(scale)
        mean, scale = jnp.concatenate([mean] * 2, axis=1), jnp.concatenate([scale] * 2, axis=1)
        columns = pl.ds(pl.multiple_of(col * WIDTH, WIDTH), WIDTH)
        values = embeds[...].astype(jnp.float32)
        values = (values - mean) * scale * gain[:, columns] + shift[:, columns]
        normed[z, x] = values.astype(jnp.bfloat16)

    for d in range(1, NX):
        plan.copy(
            f"sx{d}", f"sx{d}", 12288, lambda: stat_x.at[x], lambda: stat_x.at[x],
            lambda d=d: stat_x.at[(x - d + NX) % NX], (), -2,
        )
    plan.step("stats_x", 0.3, stats_x, [f"sx{d}" for d in range(1, NX)], -2)
    for d in range(1, NZ):
        plan.copy(
            f"sz{d}", f"sz{d}", 12288, lambda: stat_z.at[z], lambda: stat_z.at[z],
            lambda d=d: stat_z.at[(z - d + NZ) % NZ], ("stats_x",), -2,
        )
    plan.step("norm", 1.0, norm, [f"sz{d}" for d in range(1, NZ)], -2)

    def weights(tag, own, slot, count, unit, gate, level):
        whole, names = (0, count), []
        gate = list(gate)
        for mark, sign in (("p", -1), ("m", 1)):
            part = (0, count // 2) if mark == "p" else (count // 2, count)
            first, second = f"{tag}.y{mark}1", f"{tag}.y{mark}2"
            plan.copy(first, "y" + mark, count * unit, own, functools.partial(slot, 0, core, whole),
                      functools.partial(slot, sign, core, whole), gate, level)
            there = functools.partial(slot, sign, core, part)
            plan.copy(second, "y" + mark, (part[1] - part[0]) * unit, there, there,
                      functools.partial(slot, 2 * sign, core, part), [first], level)
            for name, offset, rows in ((first, sign, whole), (second, 2 * sign, part)):
                here = functools.partial(slot, offset, core, rows)
                plan.copy(name + "c", "c", (rows[1] - rows[0]) * unit, here, here,
                          functools.partial(slot, offset, 1 - core, rows), [name], level)
                names += [name, name + "c"]
        plan.copy(tag + ".c", "c", count * unit, own, functools.partial(slot, 0, core, whole),
                  functools.partial(slot, 0, 1 - core, whole), gate, level)
        return names + [tag + ".c"]

    def wide_slot(head, piece, dy, their_core, rows):
        r = 2 * ((y + dy + NY) % NY) + their_core
        return wide.at[r, head, pl.ds(piece * QROWS + rows[0], rows[1] - rows[0]), :]

    def last_slot(head, dy, their_core, rows):
        r = 2 * ((y + dy + NY) % NY) + their_core
        return last.at[r, head, pl.ds(rows[0], rows[1] - rows[0])]

    need_w, gates = {}, [[], []]
    for head in range(2):
        for piece in range(WQ):
            tag = f"w{head}{piece}"
            own = lambda head=head, piece=piece: w_qkv.at[pl.ds(piece * QROWS, QROWS), pl.ds(head * 384, 384)]
            need_w[head, piece] = weights(
                tag, own, functools.partial(wide_slot, head, piece), QROWS, 768, gates[-2], 0
            )
            gates.append([tag + ".yp1", tag + ".ym1"])
    need_o = {}
    for head in range(2):
        tag = f"o{head}"
        own = lambda head=head: w_out.at[:, head]
        need_o[head] = weights(tag, own, functools.partial(last_slot, head), 4, HEAD * WIDTH * 2, gates[-2], 0)
        gates.append([tag + ".yp1", tag + ".ym1"])

    def normed_slot(dz, dx, rows):
        return normed.at[(z + dz + NZ) % NZ, (x + dx + NX) % NX, pl.ds(rows[0], rows[1] - rows[0]), :]

    need_e = gather(plan, "e", normed_slot, WIDTH * 2, ["norm"], 0)

    def project(head, offset):
        r = (z + offset) % NZ
        left = jnp.concatenate([normed[r, i] for i in range(NX)], axis=1)
        product = jnp.dot(left, wide[r, head], preferred_element_type=jnp.float32)
        if offset == 0:
            total[...] = product
        else:
            total[...] += product

    def project_piece(piece):
        def body(r, carry):
            rows = pl.ds(piece * QROWS, QROWS)
            total[...] += jnp.dot(normed[r, piece], wide[r, 1, rows, :], preferred_element_type=jnp.float32)
            return carry

        if piece == 0:
            total[...] = jnp.zeros_like(total)
        lax.fori_loop(0, 8, body, 0)

    def attend(head):
        qkv = total[...].astype(jnp.bfloat16)
        for s in range(TOK // SEQ):
            part = qkv[s * SEQ:(s + 1) * SEQ]
            query, keys, vals = part[:, :HEAD], part[:, HEAD:2 * HEAD], part[:, 2 * HEAD:]
            scores = lax.dot_general(query, keys, (((1,), (1,)), ((), ())), preferred_element_type=jnp.float32)
            scores = scores * (HEAD ** -0.5)
            expo = jnp.exp(scores - jnp.max(scores, axis=-1, keepdims=True))
            probs = (expo / jnp.sum(expo, axis=-1, keepdims=True)).astype(jnp.bfloat16)
            mixed = jnp.dot(probs, vals, preferred_element_type=jnp.float32)
            ctx[head, z, x, pl.ds(s * SEQ, SEQ), :] = mixed.astype(jnp.bfloat16)

    def output(head, offset):
        r = (z + offset) % NZ
        left = jnp.concatenate([ctx[head, r, i] for i in range(NX)], axis=1)
        right = last[r, head].reshape(NX * HEAD, WIDTH)
        product = jnp.dot(left, right, preferred_element_type=jnp.float32)
        if head == 0 and offset == 0:
            sums[...] = product + out_bias[...]
        else:
            sums[...] += product

    walk = [0, 1, 7, 2, 6, 3, 5, 4]
    w0 = [name for piece in range(WQ) for name in need_w[0, piece]]
    before = []
    for offset in walk:
        plan.step(f"p0{offset}", 0.7, functools.partial(project, 0, offset), w0 + need_e[offset] + before, 1)
        before = [f"p0{offset}"]
    plan.step("a0", 1.5, functools.partial(attend, 0), before, 1)
    before = ["a0"] + [name for offset in walk for name in need_e[offset]]
    for piece in range(WQ):
        plan.step(f"p1{piece}", 1.3, functools.partial(project_piece, piece), need_w[1, piece] + before, 1)
        before = [f"p1{piece}"]
    plan.step("a1", 1.5, functools.partial(attend, 1), before, 1)

    for head in range(2):
        def ctx_slot(dz, dx, rows, head=head):
            return ctx.at[head, (z + dz + NZ) % NZ, (x + dx + NX) % NX, pl.ds(rows[0], rows[1] - rows[0]), :]

        need_c = gather(plan, f"c{head}", ctx_slot, HEAD * 2, [f"a{head}"], 0)
        before = [f"f{head - 1}{walk[-1]}"] if head else []
        for offset in walk:
            plan.step(
                f"f{head}{offset}", 0.3, functools.partial(output, head, offset),
                need_o[head] + need_c[offset] + before, 2,
            )
            before = [f"f{head}{offset}"]

    rate = dict(x=49e3, y=49e3, z=49e3, c=500e3, s=49e3)
    lag = dict(x=1.6, y=1.6, z=1.6, c=1.0, s=4.0)
    order = plan.order(rate, lag)

    def make(item, landed=False):
        index = item["index"]
        return pltpu.make_async_remote_copy(
            src_ref=(item["landed"] if landed else item["src"])(),
            dst_ref=(item["landed"] if landed else item["dst"])(),
            send_sem=send_sem.at[index], recv_sem=recv_sem.at[index],
            device_id=near[item["link"]], device_id_type=MESH,
        )

    barrier = pltpu.get_barrier_semaphore()
    partners = {k: v for k, v in near.items() if k not in ("sx1", "sx3", "sz1", "sz7")}
    for device in partners.values():
        pl.semaphore_signal(barrier, inc=1, device_id=device, device_id_type=MESH)
    own = [
        pltpu.make_async_copy(w_qkv.at[:, pl.ds(0, 384)], wide.at[row, 0], own_sem.at[0]),
        pltpu.make_async_copy(w_qkv.at[:, pl.ds(384, 384)], wide.at[row, 1], own_sem.at[1]),
        pltpu.make_async_copy(w_out.at[:, 0], last.at[row, 0], own_sem.at[2]),
        pltpu.make_async_copy(w_out.at[:, 1], last.at[row, 1], own_sem.at[3]),
    ]
    for item in own:
        item.start()
    stats_own()
    pl.semaphore_wait(barrier, len(partners))

    seen = set()
    used_own = False
    for name in order:
        item = plan.copies.get(name) or plan.steps[name]
        for need in item["needs"]:
            if need in plan.copies and need not in seen:
                seen.add(need)
                make(plan.copies[need], landed=True).wait_recv()
        if name in plan.copies:
            make(item).start()
        else:
            if name[0] == "p" and not used_own:
                used_own = True
                for copy in own:
                    copy.wait()
            item["run"]()
    for name, item in plan.copies.items():
        if name not in seen:
            make(item, landed=True).wait_recv()
    for item in plan.copies.values():
        make(item).wait_send()
    out[...] = sums[...].astype(jnp.bfloat16)


COPIES = 3 + 7 + 9 * (2 * WQ + 2) + 3 * (4 + 8 + 4 * 8 + 8 * 4)


def on_device(embeds, ln_gain, ln_bias, w_qkv, w_out, out_bias):
    vmem = pl.BlockSpec(memory_space=pltpu.VMEM)
    anywhere = pl.BlockSpec(memory_space=pl.ANY)
    bf16, f32 = jnp.bfloat16, jnp.float32
    return pl.pallas_call(
        kernel,
        out_shape=jax.ShapeDtypeStruct((TOK, WIDTH), bf16),
        in_specs=[vmem, vmem, vmem, anywhere, anywhere, vmem],
        out_specs=vmem,
        scratch_shapes=[
            pltpu.VMEM((NZ, NX, TOK, WIDTH), bf16),
            pltpu.VMEM((8, 2, 1024, 384), bf16),
            pltpu.VMEM((8, 2, NX, HEAD, WIDTH), bf16),
            pltpu.VMEM((2, NZ, NX, TOK, HEAD), bf16),
            pltpu.VMEM((TOK, 384), f32),
            pltpu.VMEM((TOK, WIDTH), f32),
            pltpu.VMEM((NX, 8, TOK), f32),
            pltpu.VMEM((NZ, 8, TOK), f32),
            pltpu.SemaphoreType.DMA((COPIES,)),
            pltpu.SemaphoreType.DMA((COPIES,)),
            pltpu.SemaphoreType.DMA((4,)),
        ],
        compiler_params=pltpu.CompilerParams(
            collective_id=0, has_side_effects=True, vmem_limit_bytes=60 * 1024 * 1024
        ),
        name="block",
    )(
        embeds, ln_gain.reshape(1, D), ln_bias.reshape(1, D), w_qkv,
        w_out.reshape(NX, 2, HEAD, WIDTH), out_bias.reshape(1, WIDTH),
    )


def solution(mesh):
    return jax.shard_map(
        on_device,
        mesh=mesh,
        in_specs=(P("row", "col"), P(), P(), P("row", "col"), P("row", "col"), P("col")),
        out_specs=P("row", "col"),
        check_vma=False,
    )
```

time: 323 us -> 115 us (0.36)
  waiting for transfers between devices: 278 us -> 0 us
  Pallas kernels: 0 us -> 113 us
  matrix products: 18.9 us -> 0 us
  between operations: 13.2 us -> 0.01 us
  other arithmetic: 8.28 us -> 0 us
    all_gather x4 -> x0, waiting for transfers between devices: 276 us -> none  [the longest x1 95.9 us: on_device(): lax.all_gather(embeds, 'col', axis=1, tiled=True).astype(jnp.float32)]
    pallas_call x0 -> x1, Pallas kernels: none -> 113 us  [on_device(): pl.pallas_call(kernel, out_shape=jax.ShapeDtypeStruct((TOK, WIDTH), bf16)...]
    dot_general x4 -> x0, matrix products: 18.5 us -> none  [the longest x1 11.6 us: on_device(): jnp.dot(left, lax.all_gather(w_qkv, 'row', axis=0, tiled=True), preferred...]
    reduce_sum x2 -> x0, other arithmetic: 8.27 us -> none  [the longest x1 4.57 us: on_device(): var = jnp.mean((values - mean) ** 2, axis=1, keepdims=True)]
  transfers between devices with their start and end apart: 4 -> 0, of which waited for: 4 -> 0; matrix products, arithmetic and copies ran while one was open for 7% -> 0% of each run, Pallas kernels for 0% -> 0%
where the time goes in v2:
time: 115 us
  Pallas kernels  113 us (98%)
  local copies, waits for them, and re-layouts  1.62 us (1%)
    pallas_call x1, Pallas kernels, on_device(): pl.pallas_call(kernel, out_shape=jax.ShapeDtypeStruct((TOK, WIDTH), bf16)...  113 us

profile of v2, /device:TPU:2, one launch (start us, length us, event | category | flops | bytes accessed | tf_op | source)
XLA Modules:
  0.0 114.8 jit_solution(14700926205834822636)
XLA Ops:
  0.0 113.2 %block.1 = bf16[384,256]{1,0:T(8,128)(2,1)} custom-call(bf16[384,256]{1,0:T(8,128)(2,1)} %embeds.1, f32[1,8192]{1,0:T(1,128)} %bitcast.5, f32[1,8192]{1,0:T(1,128)} %bitcast.6, bf16[1024,768]{1,0:T(8,128)(2,1)} %w_qkv.1, bf16[4,2,128,256]{3,2,1,0:T(8,128)(2,1)} %bitcast.4, f32[1,256]{1,0:T(1,128)} %bitcast.7), custom_call_target="tpu_custom_call" | custom-call | tf_op jit(solution)/shard_map/block/pallas_call | solution.py:356
  113.2 1.6 %copy.8 = bf16[384,256]{1,0:T(8,128)(2,1)} copy(bf16[384,256]{1,0:T(8,128)(2,1)} %block.1) | data formatting | bytes 393216

commit v3 on v2

v3 whole, which is shorter than its diff:
```python
import functools
import heapq

import jax
import jax.numpy as jnp
from jax import lax
from jax.experimental import pallas as pl
from jax.experimental.pallas import tpu as pltpu
from jax.sharding import PartitionSpec as P

D = 8192
SEQ = 128
HEAD = 128
TOK = 384
WIDTH = 256
NX, NY, NZ = 4, 4, 8
EARLY = ((0, 96, 256), (256, 320, 384))
LATE = ((0, 96, 256), (256, 320, 384))
AHEAD = 3
WQ = 8
QROWS = 1024 // WQ
MESH = pl.DeviceIdType.MESH


class Plan:
    def __init__(self):
        self.copies = {}
        self.groups = {}
        self.steps = {}

    def copy(self, name, link, size, src, dst, group, sent, needs=(), level=0):
        self.copies[name] = dict(
            link=link, size=size, src=src, dst=dst, group=group, sent=sent, needs=tuple(needs), level=level
        )
        if group not in self.groups:
            self.groups[group] = dict(index=len(self.groups), size=0)
        self.groups[group]["size"] += size

    def step(self, name, cost, run, needs=(), level=0):
        self.steps[name] = dict(cost=cost, run=run, needs=tuple(needs), level=level)

    def order(self, rate, lag):
        now, when, free, left = 0.0, {}, {}, {}
        for item in self.copies.values():
            left[item["group"]] = left.get(item["group"], 0) + 1
        landed = {}
        waiting = {**self.copies, **self.steps}
        result = []
        while waiting:
            best = None
            for name, item in waiting.items():
                times = [when.get(need) for need in item["needs"]]
                if any(t is None for t in times):
                    continue
                ready = max(times, default=0.0)
                if "link" in item:
                    ready = max(ready, free.get(item["link"], 0.0) - QUEUE)
                key = (max(ready - item.get("eager", 0.0), now), item["level"], ready, name in self.steps)
                if best is None or key < best[0]:
                    best = (key, name)
            key, name = best
            item = waiting.pop(name)
            now = max(now, key[2])
            result.append(name)
            if name in self.steps:
                now += item["cost"]
                when[name] = now
            else:
                now += 0.01
                link, group = item["link"], item["group"]
                begin = max(now, free.get(link, 0.0))
                free[link] = begin + item["size"] / rate[link[0]]
                landed[group] = max(landed.get(group, 0.0), free[link] + lag[link[0]])
                left[group] -= 1
                if not left[group]:
                    when[group] = landed[group]
        self.when = when
        return result


def halves(rows, mark):
    low, high = rows
    middle = (low + high) // 2
    return (low, middle) if mark == "p" else (middle, high)


def ring(plan, axis, n, tag, classes, slot, rows, size, needs, level, after=0, last=None):
    done = {0: list(needs)}
    for hop in range(1, n // 2 + 1):
        group = last if last and hop == n // 2 else f"{tag}_{hop}"
        for place in classes:
            for sign, mark in ((-1, "p"), (1, "m")):
                part = halves(rows, mark) if hop == n // 2 else rows
                place_of = (place, sign * (hop - 1), part)
                plan.copy(
                    f"{tag}_{place}{mark}{hop}", axis + mark, size * (part[1] - part[0]),
                    functools.partial(slot, *place_of, True), functools.partial(slot, *place_of, False), group,
                    tag[:2], done[hop - 1], level - HOP * (n // 2 - hop + after),
                )
        done[hop] = [group]
    return done


def gather(plan, tag, slot, part, size, needs, level, merged=0):
    first, second = part[:2], part[1:]
    found = {distance: [] for distance in range(NZ // 2 + 1)}
    ends = lambda distance: f"{tag}z" if distance < merged else None
    along_x = lambda place, offset, rows, src: slot(place, offset, rows, src)
    along_z = lambda place, offset, rows, src: slot(offset, place, rows, src)
    pairs = lambda distance, n: sorted({distance, (n - distance) % n})
    across = ring(plan, "x", NX, tag + "a", [0], along_x, first, size, needs, level, NZ // 2)
    along = ring(plan, "z", NZ, tag + "b", [0], along_z, second, size, needs, level, NX // 2)
    for distance in range(NX // 2 + 1):
        done = ring(plan, "z", NZ, f"{tag}a{distance}", pairs(distance, NX), along_z, first, size, across[distance],
                    level, 0, ends(NZ // 2) or f"{tag}al")
        for hop, names in done.items():
            found[hop] += names
    for distance in range(NZ // 2 + 1):
        done = ring(plan, "x", NX, f"{tag}b{distance}", pairs(distance, NZ), along_x, second, size, along[distance],
                    level, 0, ends(distance))
        for names in done.values():
            found[distance] += names
    return found


def to_columns(row):
    wide = jnp.transpose(jnp.broadcast_to(row, (128, TOK)))
    return jnp.concatenate([wide] * (WIDTH // 128), axis=1)


def kernel(embeds, gain, shift, w_qkv, w_out, out_bias, out, raw, normed, wide, last, ctx, total, sums, mean_cols,
           scale_cols, stat_x, stat_z, send_sem, recv_sem, own_sem):
    row, col = lax.axis_index("row"), lax.axis_index("col")
    y, core = row // 2, row % 2
    z, x = col // NX, col % NX

    def at(dx=0, dy=0, dz=0, other=0):
        their_core = 1 - core if other else core
        return (2 * ((y + dy + NY) % NY) + their_core, NX * ((z + dz + NZ) % NZ) + (x + dx + NX) % NX)

    near = dict(
        xp=at(dx=1), xm=at(dx=-1), yp=at(dy=1), ym=at(dy=-1), zp=at(dz=1), zm=at(dz=-1), c=at(other=1)
    )
    for d in range(1, NX):
        near[f"sx{d}"] = at(dx=d)
    for d in range(1, NZ):
        near[f"sz{d}"] = at(dz=d)

    plan = Plan()

    lines = lax.broadcasted_iota(jnp.int32, (8, TOK), 0)

    def pack(total_, spread):
        return jnp.where(lines == 0, total_, jnp.where(lines == 1, spread, 0.0))

    def merge(stats, n, count):
        totals = [stats[i][0:1] for i in range(n)]
        full = functools.reduce(jnp.add, totals)
        mean = full * (1.0 / (n * count))
        spread = functools.reduce(jnp.add, [stats[i][1:2] for i in range(n)])
        apart = functools.reduce(jnp.add, [(t * (1.0 / count) - mean) ** 2 for t in totals])
        return full, mean, spread + count * apart

    def stats_own():
        values = embeds[...].astype(jnp.float32)
        summed = jnp.sum(values, axis=1, keepdims=True)
        apart = values - summed * (1.0 / WIDTH)
        spread = jnp.sum(apart * apart, axis=1, keepdims=True)
        lane = lax.broadcasted_iota(jnp.int32, (TOK, 128), 1)
        both = jnp.where(lane == 0, summed, jnp.where(lane == 1, spread, 0.0))
        stat_x[x] = jnp.transpose(both)[0:8]
        raw[col] = embeds[...]

    def stats_x():
        full, _, spread = merge(stat_x, NX, WIDTH)
        stat_z[z] = pack(full, spread)

    def stats_all():
        _, mean, spread = merge(stat_z, NZ, NX * WIDTH)
        mean_cols[...] = to_columns(mean)
        scale_cols[...] = to_columns(lax.rsqrt(spread * (1.0 / D) + 1e-05))

    plan.step("stats_own", 0.8, stats_own, [], 0.5)
    for d in range(1, NX):
        plan.copy(f"sx{d}", f"sx{d}", 12288, lambda: stat_x.at[x], lambda: stat_x.at[x], "sx", "sx", ["stats_own"], -2)
    plan.step("stats_x", 0.1, stats_x, ["sx"], -2)
    for d in range(1, NZ):
        plan.copy(f"sz{d}", f"sz{d}", 12288, lambda: stat_z.at[z], lambda: stat_z.at[z], "sz", "sz", ["stats_x"], -2)
    plan.step("stats_all", 0.2, stats_all, ["sz"], -2)

    def weights(tag, own, slot, count, unit, gate, from_core):
        whole = (0, count)
        ends = [f"{tag}_1", f"{tag}_2", from_core]
        for mark, sign in (("p", -1), ("m", 1)):
            part = halves(whole, mark)
            plan.copy(f"{tag}_{mark}1", "y" + mark, count * unit, own, functools.partial(slot, 0, whole), ends[0],
                      tag[0], gate, -1)
            near_part, near_all = functools.partial(slot, sign, part), functools.partial(slot, sign, whole)
            far_part = functools.partial(slot, 2 * sign, part)
            plan.copy(f"{tag}_{mark}2", "y" + mark, (part[1] - part[0]) * unit, near_part, near_part, ends[1], tag[0],
                      ends[:1], -1)
            plan.copy(f"{tag}_{mark}1c", "c", count * unit, near_all, near_all, from_core, tag[0], ends[:1], -1)
            plan.copy(f"{tag}_{mark}2c", "c", (part[1] - part[0]) * unit, far_part, far_part, from_core, tag[0],
                      ends[1:2], -1)
        plan.copy(f"{tag}_c", "c", count * unit, own, functools.partial(slot, 0, whole), from_core, tag[0], gate, -1)
        return ends

    def wide_slot(head, piece, dy, rows):
        return wide.at[2 * ((y + dy + NY) % NY) + core, head, pl.ds(piece * QROWS + rows[0], rows[1] - rows[0]), :]

    def last_slot(head, dy, rows):
        return last.at[2 * ((y + dy + NY) % NY) + core, head, pl.ds(rows[0], rows[1] - rows[0])]

    need_w, gates = {}, [[]] * AHEAD
    first = [f"w0{WQ - 1}_1"]
    for head in range(2):
        for piece in range(WQ):
            own = lambda head=head, piece=piece: w_qkv.at[pl.ds(piece * QROWS, QROWS), pl.ds(head * 384, 384)]
            need_w[head, piece] = weights(
                f"w{head}{piece}", own, functools.partial(wide_slot, head, piece), QROWS, 768,
                first if head and piece > AHEAD and FREE else gates[-AHEAD], f"w1{piece * NX // WQ}_c" if head else "w0_c",
            )
            gates.append([f"w{head}{piece}_1"])
    need_o = {}
    for head in range(2):
        own = lambda head=head: w_out.at[:, head]
        need_o[head] = weights(
            f"o{head}", own, functools.partial(last_slot, head), 4, HEAD * WIDTH * 2, [f"w1{WQ - 1}_1"], f"o{head}_c"
        )

    def raw_slot(dz, dx, rows, src):
        if src and dz == 0 and dx == 0:
            return embeds.at[pl.ds(rows[0], rows[1] - rows[0]), :]
        return raw.at[NX * ((z + dz + NZ) % NZ) + (x + dx + NX) % NX, pl.ds(rows[0], rows[1] - rows[0]), :]

    need_e = [gather(plan, f"e{i}", raw_slot, part, WIDTH * 2, [], LEVELS[0]) for i, part in enumerate(EARLY)]

    def normalize(part, distance):
        rows = pl.ds(part[0], part[2] - part[0])
        for offset in sorted({distance, (NZ - distance) % NZ}):
            r = (z + offset) % NZ

            def body(i, carry, r=r):
                columns = pl.ds(pl.multiple_of((NX * r + i) * WIDTH, WIDTH), WIDTH)
                values = raw[NX * r + i, rows, :].astype(jnp.float32)
                values = (values - mean_cols[rows, :]) * scale_cols[rows, :] * gain[:, columns] + shift[:, columns]
                normed[r, i, rows, :] = values.astype(jnp.bfloat16)
                return carry

            lax.fori_loop(0, NX, body, 0)

    def project(part, distance):
        rows = pl.ds(part[0], part[2] - part[0])
        for offset in sorted({distance, (NZ - distance) % NZ}):
            r = (z + offset) % NZ
            left = jnp.concatenate([normed[r, i, rows, :] for i in range(NX)], axis=1)
            product = jnp.dot(left, wide[r, 0], preferred_element_type=jnp.float32)
            if offset == 0:
                total[rows, :] = product
            else:
                total[rows, :] += product

    def project_piece(piece):
        rows = pl.ds(piece * WIDTH, WIDTH)
        for some in (range(0, 4), range(4, 8)):
            left = jnp.concatenate([normed[r, piece] for r in some], axis=1)
            right = jnp.concatenate([wide[r, 1, rows, :] for r in some], axis=0)
            product = jnp.dot(left, right, preferred_element_type=jnp.float32)
            if piece == 0 and some[0] == 0:
                total[...] = product
            else:
                total[...] += product

    def attend(head, low, high):
        for s in range(low // SEQ, high // SEQ):
            part = total[pl.ds(s * SEQ, SEQ), :].astype(jnp.bfloat16)
            query, keys, vals = part[:, :HEAD], part[:, HEAD:2 * HEAD], part[:, 2 * HEAD:]
            scores = lax.dot_general(query, keys, (((1,), (1,)), ((), ())), preferred_element_type=jnp.float32)
            scores = scores * (HEAD ** -0.5)
            expo = jnp.exp(scores - jnp.max(scores, axis=-1, keepdims=True))
            probs = (expo / jnp.sum(expo, axis=-1, keepdims=True)).astype(jnp.bfloat16)
            mixed = jnp.dot(probs, vals, preferred_element_type=jnp.float32)
            ctx[head, col, pl.ds(s * SEQ, SEQ), :] = mixed.astype(jnp.bfloat16)

    def output(head, distance):
        product = None
        for offset in sorted({distance, (NZ - distance) % NZ}):
            r = (z + offset) % NZ
            left = jnp.concatenate([ctx[head, NX * r + i] for i in range(NX)], axis=1)
            right = last[r, head].reshape(NX * HEAD, WIDTH)
            more = jnp.dot(left, right, preferred_element_type=jnp.float32)
            product = more if product is None else product + more
        if head == 0 and distance == 0:
            sums[...] = product + out_bias[...]
        else:
            sums[...] += product

    distances = range(NZ // 2 + 1)
    w0 = sorted({name for piece in range(WQ) for name in need_w[0, piece]})
    before = ["own"]
    plan.step("own", 0.01, lambda: [copy.wait() for copy in own_copies], ["stats_all"], 1)
    for i, part in enumerate(EARLY):
        share = (part[2] - part[0]) / TOK
        for d in distances:
            many = share if d in (0, NZ // 2) else 2 * share
            plan.step(f"n{i}{d}", 0.3 * many, functools.partial(normalize, part, d), ["stats_all", "own"] + need_e[i][d], 1)
            plan.step(f"p{i}{d}", 0.6 * many, functools.partial(project, part, d), w0 + [f"n{i}{d}"] + before, 1)
            before = [f"p{i}{d}"]
        plan.step(f"a{i}", 0.9 * share, functools.partial(attend, 0, part[0], part[2]), before, 0)
    before = [f"a{len(EARLY) - 1}"]
    for piece in range(NX):
        parts = range(piece * WQ // NX, (piece + 1) * WQ // NX)
        needs = [name for part in parts for name in need_w[1, part]]
        plan.step(f"q{piece}", 1.2, functools.partial(project_piece, piece), needs + before, 1)
        before = [f"q{piece}"]
        plan.steps[f"q{piece}"]["eager"] = EAGER if piece == NX - 1 else 0.0
    plan.step("b0", 0.8, functools.partial(attend, 1, 0, TOK), before, 0)
    plan.steps["b0"]["eager"] = EAGER

    for head, parts in enumerate((EARLY, LATE)):
        def ctx_slot(dz, dx, rows, src, head=head):
            place = NX * ((z + dz + NZ) % NZ) + (x + dx + NX) % NX
            return ctx.at[head, place, pl.ds(rows[0], rows[1] - rows[0]), :]

        need_c = [
            gather(plan, f"{'cd'[head]}{i}", ctx_slot, part, HEAD * 2, ["b0" if head else f"a{i}"], LEVELS[1 + head], MERGED[head])
            for i, part in enumerate(parts)
        ]
        before = [f"f{head - 1}{NZ // 2}"] if head else []
        for d in distances:
            many = 1 if d in (0, NZ // 2) else 2
            plan.step(
                f"f{head}{d}", 0.21 * many, functools.partial(output, head, d),
                need_o[head] + [name for need in need_c for name in need[d]] + before, 2,
            )
            before = [f"f{head}{d}"]

    order = plan.order(RATE, LAG)
    sends = dict(
        sx=stat_x.at[pl.ds(0, NX - 1)], sz=stat_z.at[pl.ds(0, NZ - 1)], w=wide.at[pl.ds(0, 7)], o=last.at[pl.ds(0, 7)]
    )
    others = pl.ds(0, NZ * NX - 1)
    for tag, buffer, parts in (("e", raw, EARLY), ("c", ctx.at[0], EARLY), ("d", ctx.at[1], LATE)):
        for i, part in enumerate(parts):
            sends[f"{tag}{i}"] = buffer.at[others, pl.ds(part[0], part[2] - part[0]), :]
    send_index = {name: i for i, name in enumerate(sends)}

    def start(item):
        pltpu.make_async_remote_copy(
            src_ref=item["src"](), dst_ref=item["dst"](), send_sem=send_sem.at[send_index[item["sent"]]],
            recv_sem=recv_sem.at[plan.groups[item["group"]]["index"]],
            device_id=near[item["link"]], device_id_type=MESH,
        ).start()

    def take(ref, sem):
        pltpu.make_async_copy(ref, ref, sem).wait()

    def of_size(size):
        rows = size // (HEAD * 2)
        for slots in range(1, NZ * NX + 1):
            if rows % (16 * slots) == 0 and rows // slots <= TOK:
                return ctx.at[0, pl.ds(0, slots), pl.ds(0, rows // slots)]
        raise ValueError(size)

    barrier = pltpu.get_barrier_semaphore()
    partners = {k: v for k, v in near.items() if k not in ("sx1", "sx3", "sz1", "sz7")}
    for device in partners.values():
        pl.semaphore_signal(barrier, inc=1, device_id=device, device_id_type=MESH)
    own_copies = [
        pltpu.make_async_copy(w_qkv.at[:, pl.ds(0, 384)], wide.at[row, 0], own_sem.at[0]),
        pltpu.make_async_copy(w_qkv.at[:, pl.ds(384, 384)], wide.at[row, 1], own_sem.at[1]),
        pltpu.make_async_copy(w_out.at[:, 0], last.at[row, 0], own_sem.at[2]),
        pltpu.make_async_copy(w_out.at[:, 1], last.at[row, 1], own_sem.at[3]),
    ]
    for item in own_copies:
        item.start()
    pl.semaphore_wait(barrier, len(partners))

    seen = set()
    for name in order:
        item = plan.copies.get(name) or plan.steps[name]
        for need in item["needs"]:
            if need in plan.groups and need not in seen:
                seen.add(need)
                group = plan.groups[need]
                take(of_size(group["size"]), recv_sem.at[group["index"]])
        if name in plan.copies:
            start(item)
        else:
            item["run"]()
    for name, ref in sends.items():
        take(ref, send_sem.at[send_index[name]])
    out[...] = sums[...].astype(jnp.bfloat16)


QUEUE = 1.5
HOP = 0.01
FREE = True
MERGED = (NZ, 3)
EAGER = 1.0
LEVELS = (0, 0, 0)
RATE = dict(x=47e3, y=45e3, z=47e3, c=500e3, s=47e3)
LAG = dict(x=1.8, y=1.8, z=1.8, c=1.0, s=8.0)
GROUPS = 2 + (2 * 2 * WQ + 1 + NX) + 6 + len(EARLY) * (26 + 26 - 5) + len(LATE) * (26 - 2)


def on_device(embeds, ln_gain, ln_bias, w_qkv, w_out, out_bias):
    vmem = pl.BlockSpec(memory_space=pltpu.VMEM)
    anywhere = pl.BlockSpec(memory_space=pl.ANY)
    bf16, f32 = jnp.bfloat16, jnp.float32
    return pl.pallas_call(
        kernel,
        out_shape=jax.ShapeDtypeStruct((TOK, WIDTH), bf16),
        in_specs=[vmem, vmem, vmem, anywhere, anywhere, vmem],
        out_specs=vmem,
        scratch_shapes=[
            pltpu.VMEM((NZ * NX, TOK, WIDTH), bf16),
            pltpu.VMEM((NZ, NX, TOK, WIDTH), bf16),
            pltpu.VMEM((8, 2, 1024, 384), bf16),
            pltpu.VMEM((8, 2, NX, HEAD, WIDTH), bf16),
            pltpu.VMEM((2, NZ * NX, TOK, HEAD), bf16),
            pltpu.VMEM((TOK, 384), f32),
            pltpu.VMEM((TOK, WIDTH), f32),
            pltpu.VMEM((TOK, WIDTH), f32),
            pltpu.VMEM((TOK, WIDTH), f32),
            pltpu.VMEM((NX, 8, TOK), f32),
            pltpu.VMEM((NZ, 8, TOK), f32),
            pltpu.SemaphoreType.DMA((4 + 2 * len(EARLY) + len(LATE),)),
            pltpu.SemaphoreType.DMA((GROUPS,)),
            pltpu.SemaphoreType.DMA((4,)),
        ],
        compiler_params=pltpu.CompilerParams(
            collective_id=0, has_side_effects=True, vmem_limit_bytes=60 * 1024 * 1024
        ),
        name="block",
    )(
        embeds, ln_gain.reshape(1, D), ln_bias.reshape(1, D), w_qkv,
        w_out.reshape(NX, 2, HEAD, WIDTH), out_bias.reshape(1, WIDTH),
    )


def solution(mesh):
    return jax.shard_map(
        on_device,
        mesh=mesh,
        in_specs=(P("row", "col"), P(), P(), P("row", "col"), P("row", "col"), P("col")),
        out_specs=P("row", "col"),
        check_vma=False,
    )
```

time: 115 us -> 101 us (0.88)
  Pallas kernels: 113 us -> 99.6 us
    pallas_call x1, Pallas kernels: 113 us -> 99.6 us  [on_device(): pl.pallas_call(kernel, out_shape=jax.ShapeDtypeStruct((TOK, WIDTH), bf16)...]
where the time goes in v3:
time: 101 us
  Pallas kernels  99.6 us (99%)
  local copies, waits for them, and re-layouts  1.62 us (2%)
    pallas_call x1, Pallas kernels, on_device(): pl.pallas_call(kernel, out_shape=jax.ShapeDtypeStruct((TOK, WIDTH), bf16)...  99.6 us

profile of v3, /device:TPU:2, one launch (start us, length us, event | category | flops | bytes accessed | tf_op | source)
XLA Modules:
  0.0 101.2 jit_solution(15899386502833251547)
XLA Ops:
  0.0 99.6 %block.1 = bf16[384,256]{1,0:T(8,128)(2,1)} custom-call(bf16[384,256]{1,0:T(8,128)(2,1)} %embeds.1, f32[1,8192]{1,0:T(1,128)} %bitcast.5, f32[1,8192]{1,0:T(1,128)} %bitcast.6, bf16[1024,768]{1,0:T(8,128)(2,1)} %w_qkv.1, bf16[4,2,128,256]{3,2,1,0:T(8,128)(2,1)} %bitcast.4, f32[1,256]{1,0:T(1,128)} %bitcast.7), custom_call_target="tpu_custom_call" | custom-call | tf_op jit(solution)/shard_map/block/pallas_call | solution.py:411
  99.6 1.6 %copy.8 = bf16[384,256]{1,0:T(8,128)(2,1)} copy(bf16[384,256]{1,0:T(8,128)(2,1)} %block.1) | data formatting | bytes 393216

commit v4 on v3

--- a/solution.py
+++ b/solution.py
@@ -17,7 +17,7 @@
 EARLY = ((0, 96, 256), (256, 320, 384))
 LATE = ((0, 96, 256), (256, 320, 384))
 AHEAD = 3
-WQ = 8
+WQ = 4
 QROWS = 1024 // WQ
 MESH = pl.DeviceIdType.MESH
 
@@ -54,7 +54,7 @@
                     continue
                 ready = max(times, default=0.0)
                 if "link" in item:
-                    ready = max(ready, free.get(item["link"], 0.0) - QUEUE)
+                    ready = max(ready, free.get(item["link"], 0.0) - QUEUE.get(item["link"][0], 99.0))
                 key = (max(ready - item.get("eager", 0.0), now), item["level"], ready, name in self.steps)
                 if best is None or key < best[0]:
                     best = (key, name)
@@ -212,13 +212,20 @@
         return last.at[2 * ((y + dy + NY) % NY) + core, head, pl.ds(rows[0], rows[1] - rows[0])]
 
     need_w, gates = {}, [[]] * AHEAD
-    first = [f"w0{WQ - 1}_1"]
+
+    def gate(head, piece):
+        if head and piece < FIRST:
+            return [f"w0{WQ - 1 - FIRST + piece}_1"]
+        if head and piece < FIRST + NEXT:
+            return [f"w0{WQ - 1}_1"]
+        return gates[-AHEAD]
+
     for head in range(2):
         for piece in range(WQ):
             own = lambda head=head, piece=piece: w_qkv.at[pl.ds(piece * QROWS, QROWS), pl.ds(head * 384, 384)]
             need_w[head, piece] = weights(
                 f"w{head}{piece}", own, functools.partial(wide_slot, head, piece), QROWS, 768,
-                first if head and piece > AHEAD and FREE else gates[-AHEAD], f"w1{piece * NX // WQ}_c" if head else "w0_c",
+                gate(head, piece), f"w1{piece * NX // WQ}_c" if head else "w0_c",
             )
             gates.append([f"w{head}{piece}_1"])
     need_o = {}
@@ -393,9 +400,10 @@
     out[...] = sums[...].astype(jnp.bfloat16)
 
 
-QUEUE = 1.5
+QUEUE = dict(x=1.5, z=1.5)
 HOP = 0.01
-FREE = True
+FIRST = 0
+NEXT = 0
 MERGED = (NZ, 3)
 EAGER = 1.0
 LEVELS = (0, 0, 0)

time: 101 us -> 98.4 us (0.974)
  Pallas kernels: 99.6 us -> 96.5 us
    pallas_call x1, Pallas kernels: 99.6 us -> 96.5 us  [on_device(): pl.pallas_call(kernel, out_shape=jax.ShapeDtypeStruct((TOK, WIDTH), bf16)...]
where the time goes in v4:
time: 98.4 us; the launch traced here: 98.1 us
  Pallas kernels  96.5 us (98%)
  local copies, waits for them, and re-layouts  1.62 us (2%)
    pallas_call x1, Pallas kernels, on_device(): pl.pallas_call(kernel, out_shape=jax.ShapeDtypeStruct((TOK, WIDTH), bf16)...  96.5 us

profile of v4, /device:TPU:2, one launch (start us, length us, event | category | flops | bytes accessed | tf_op | source)
XLA Modules:
  0.0 98.1 jit_solution(4055876809246765860)
XLA Ops:
  0.0 96.5 %block.1 = bf16[384,256]{1,0:T(8,128)(2,1)} custom-call(bf16[384,256]{1,0:T(8,128)(2,1)} %embeds.1, f32[1,8192]{1,0:T(1,128)} %bitcast.5, f32[1,8192]{1,0:T(1,128)} %bitcast.6, bf16[1024,768]{1,0:T(8,128)(2,1)} %w_qkv.1, bf16[4,2,128,256]{3,2,1,0:T(8,128)(2,1)} %bitcast.4, f32[1,256]{1,0:T(1,128)} %bitcast.7), custom_call_target="tpu_custom_call" | custom-call | tf_op jit(solution)/shard_map/block/pallas_call | solution.py:419
  96.5 1.6 %copy.8 = bf16[384,256]{1,0:T(8,128)(2,1)} copy(bf16[384,256]{1,0:T(8,128)(2,1)} %block.1) | data formatting | bytes 393216

commit v5 on v4

--- a/solution.py
+++ b/solution.py
@@ -70,7 +70,7 @@
                 link, group = item["link"], item["group"]
                 begin = max(now, free.get(link, 0.0))
                 free[link] = begin + item["size"] / rate[link[0]]
-                landed[group] = max(landed.get(group, 0.0), free[link] + lag[link[0]])
+                landed[group] = max(landed.get(group, 0.0), free[link] + lag[link[0]] + (SLACK if item["size"] == STAT else 0.0))
                 left[group] -= 1
                 if not left[group]:
                     when[group] = landed[group]
@@ -128,7 +128,7 @@
     return jnp.concatenate([wide] * (WIDTH // 128), axis=1)
 
 
-def kernel(embeds, gain, shift, w_qkv, w_out, out_bias, out, raw, normed, wide, last, ctx, total, sums, mean_cols,
+def kernel(embeds, gain_in, shift_in, w_qkv, w_out, bias_in, out, gain, shift, out_bias, raw, normed, wide, last, ctx, total, sums, mean_cols,
            scale_cols, stat_x, stat_z, send_sem, recv_sem, own_sem):
     row, col = lax.axis_index("row"), lax.axis_index("col")
     y, core = row // 2, row % 2
@@ -141,10 +141,6 @@
     near = dict(
         xp=at(dx=1), xm=at(dx=-1), yp=at(dy=1), ym=at(dy=-1), zp=at(dz=1), zm=at(dz=-1), c=at(other=1)
     )
-    for d in range(1, NX):
-        near[f"sx{d}"] = at(dx=d)
-    for d in range(1, NZ):
-        near[f"sz{d}"] = at(dz=d)
 
     plan = Plan()
 
@@ -162,14 +158,14 @@
         return full, mean, spread + count * apart
 
     def stats_own():
-        values = embeds[...].astype(jnp.float32)
+        own_copies[-1].wait()
+        values = raw[col].astype(jnp.float32)
         summed = jnp.sum(values, axis=1, keepdims=True)
         apart = values - summed * (1.0 / WIDTH)
         spread = jnp.sum(apart * apart, axis=1, keepdims=True)
         lane = lax.broadcasted_iota(jnp.int32, (TOK, 128), 1)
         both = jnp.where(lane == 0, summed, jnp.where(lane == 1, spread, 0.0))
         stat_x[x] = jnp.transpose(both)[0:8]
-        raw[col] = embeds[...]
 
     def stats_x():
         full, _, spread = merge(stat_x, NX, WIDTH)
@@ -181,12 +177,17 @@
         scale_cols[...] = to_columns(lax.rsqrt(spread * (1.0 / D) + 1e-05))
 
     plan.step("stats_own", 0.8, stats_own, [], 0.5)
-    for d in range(1, NX):
-        plan.copy(f"sx{d}", f"sx{d}", 12288, lambda: stat_x.at[x], lambda: stat_x.at[x], "sx", "sx", ["stats_own"], -2)
-    plan.step("stats_x", 0.1, stats_x, ["sx"], -2)
-    for d in range(1, NZ):
-        plan.copy(f"sz{d}", f"sz{d}", 12288, lambda: stat_z.at[z], lambda: stat_z.at[z], "sz", "sz", ["stats_x"], -2)
-    plan.step("stats_all", 0.2, stats_all, ["sz"], -2)
+    def stat_ring(axis, n, stats, place, needs):
+        for hop in range(1, n // 2 + 1):
+            for sign, mark in ((-1, "p"), (1, "m")):
+                if mark == "p" or hop < n // 2:
+                    ref = lambda held=(place + sign * (hop - 1) + n) % n: stats.at[held]
+                    plan.copy(f"s{axis}{mark}{hop}", axis + mark, STAT, ref, ref, f"s{axis}_{hop}", f"s{axis}", needs, -2)
+            needs = [f"s{axis}_{hop}"]
+        return [f"s{axis}_{hop}" for hop in range(1, n // 2 + 1)]
+
+    plan.step("stats_x", 0.1, stats_x, stat_ring("x", NX, stat_x, x, ["stats_own"]), -2)
+    plan.step("stats_all", 0.2, stats_all, stat_ring("z", NZ, stat_z, z, ["stats_x"]), 0.5)
 
     def weights(tag, own, slot, count, unit, gate, from_core):
         whole = (0, count)
@@ -305,7 +306,7 @@
     distances = range(NZ // 2 + 1)
     w0 = sorted({name for piece in range(WQ) for name in need_w[0, piece]})
     before = ["own"]
-    plan.step("own", 0.01, lambda: [copy.wait() for copy in own_copies], ["stats_all"], 1)
+    plan.step("own", 0.01, lambda: [copy.wait() for copy in own_copies[:-1]], ["stats_all"], 1)
     for i, part in enumerate(EARLY):
         share = (part[2] - part[0]) / TOK
         for d in distances:
@@ -318,7 +319,7 @@
     for piece in range(NX):
         parts = range(piece * WQ // NX, (piece + 1) * WQ // NX)
         needs = [name for part in parts for name in need_w[1, part]]
-        plan.step(f"q{piece}", 1.2, functools.partial(project_piece, piece), needs + before, 1)
+        plan.step(f"q{piece}", 1.6, functools.partial(project_piece, piece), needs + before, 1)
         before = [f"q{piece}"]
         plan.steps[f"q{piece}"]["eager"] = EAGER if piece == NX - 1 else 0.0
     plan.step("b0", 0.8, functools.partial(attend, 1, 0, TOK), before, 0)
@@ -370,18 +371,21 @@
         raise ValueError(size)
 
     barrier = pltpu.get_barrier_semaphore()
-    partners = {k: v for k, v in near.items() if k not in ("sx1", "sx3", "sz1", "sz7")}
-    for device in partners.values():
+    for device in near.values():
         pl.semaphore_signal(barrier, inc=1, device_id=device, device_id_type=MESH)
     own_copies = [
         pltpu.make_async_copy(w_qkv.at[:, pl.ds(0, 384)], wide.at[row, 0], own_sem.at[0]),
         pltpu.make_async_copy(w_qkv.at[:, pl.ds(384, 384)], wide.at[row, 1], own_sem.at[1]),
         pltpu.make_async_copy(w_out.at[:, 0], last.at[row, 0], own_sem.at[2]),
         pltpu.make_async_copy(w_out.at[:, 1], last.at[row, 1], own_sem.at[3]),
+        pltpu.make_async_copy(gain_in, gain, own_sem.at[4]),
+        pltpu.make_async_copy(shift_in, shift, own_sem.at[5]),
+        pltpu.make_async_copy(bias_in, out_bias, own_sem.at[6]),
+        pltpu.make_async_copy(embeds, raw.at[col], own_sem.at[7]),
     ]
     for item in own_copies:
         item.start()
-    pl.semaphore_wait(barrier, len(partners))
+    pl.semaphore_wait(barrier, len(near))
 
     seen = set()
     for name in order:
@@ -405,11 +409,13 @@
 FIRST = 0
 NEXT = 0
 MERGED = (NZ, 3)
-EAGER = 1.0
+EAGER = 2.0
+STAT = 8 * TOK * 4
+SLACK = 0.5
 LEVELS = (0, 0, 0)
-RATE = dict(x=47e3, y=45e3, z=47e3, c=500e3, s=47e3)
+RATE = dict(x=47e3, y=47e3, z=47e3, c=500e3, s=47e3)
 LAG = dict(x=1.8, y=1.8, z=1.8, c=1.0, s=8.0)
-GROUPS = 2 + (2 * 2 * WQ + 1 + NX) + 6 + len(EARLY) * (26 + 26 - 5) + len(LATE) * (26 - 2)
+GROUPS = 6 + (2 * 2 * WQ + 1 + NX) + 6 + len(EARLY) * (26 + 26 - 5) + len(LATE) * (26 - 2)
 
 
 def on_device(embeds, ln_gain, ln_bias, w_qkv, w_out, out_bias):
@@ -419,9 +425,12 @@
     return pl.pallas_call(
         kernel,
         out_shape=jax.ShapeDtypeStruct((TOK, WIDTH), bf16),
-        in_specs=[vmem, vmem, vmem, anywhere, anywhere, vmem],
+        in_specs=[anywhere] * 6,
         out_specs=vmem,
         scratch_shapes=[
+            pltpu.VMEM((1, D), f32),
+            pltpu.VMEM((1, D), f32),
+            pltpu.VMEM((1, WIDTH), f32),
             pltpu.VMEM((NZ * NX, TOK, WIDTH), bf16),
             pltpu.VMEM((NZ, NX, TOK, WIDTH), bf16),
             pltpu.VMEM((8, 2, 1024, 384), bf16),
@@ -435,7 +444,7 @@
             pltpu.VMEM((NZ, 8, TOK), f32),
             pltpu.SemaphoreType.DMA((4 + 2 * len(EARLY) + len(LATE),)),
             pltpu.SemaphoreType.DMA((GROUPS,)),
-            pltpu.SemaphoreType.DMA((4,)),
+            pltpu.SemaphoreType.DMA((8,)),
         ],
         compiler_params=pltpu.CompilerParams(
             collective_id=0, has_side_effects=True, vmem_limit_bytes=60 * 1024 * 1024

time: 98.4 us -> 96.3 us (0.979)
  Pallas kernels: 96.5 us -> 94.5 us
    pallas_call x1, Pallas kernels: 96.5 us -> 94.5 us  [on_device(): pl.pallas_call(kernel, out_shape=jax.ShapeDtypeStruct((TOK, WIDTH), bf16)...]
where the time goes in v5:
time: 96.3 us; the launch traced here: 96.2 us
  Pallas kernels  94.5 us (98%)
  local copies, waits for them, and re-layouts  1.62 us (2%)
    pallas_call x1, Pallas kernels, on_device(): pl.pallas_call(kernel, out_shape=jax.ShapeDtypeStruct((TOK, WIDTH), bf16)...  94.5 us

profile of v5, /device:TPU:2, one launch (start us, length us, event | category | flops | bytes accessed | tf_op | source)
XLA Modules:
  0.0 96.2 jit_solution(12900709883370205927)
XLA Ops:
  0.0 94.5 %block.1 = bf16[384,256]{1,0:T(8,128)(2,1)} custom-call(bf16[384,256]{1,0:T(8,128)(2,1)} %embeds.1, f32[1,8192]{1,0:T(1,128)} %bitcast.5, f32[1,8192]{1,0:T(1,128)} %bitcast.6, bf16[1024,768]{1,0:T(8,128)(2,1)} %w_qkv.1, bf16[4,2,128,256]{3,2,1,0:T(8,128)(2,1)} %bitcast.4, f32[1,256]{1,0:T(1,128)} %bitcast.7), custom_call_target="tpu_custom_call" | custom-call | tf_op jit(solution)/shard_map/block/pallas_call | solution.py:425
  94.5 1.6 %copy.8 = bf16[384,256]{1,0:T(8,128)(2,1)} copy(bf16[384,256]{1,0:T(8,128)(2,1)} %block.1) | data formatting | bytes 393216

commit v6 on v5

--- a/solution.py
+++ b/solution.py
@@ -413,7 +413,7 @@
 STAT = 8 * TOK * 4
 SLACK = 0.5
 LEVELS = (0, 0, 0)
-RATE = dict(x=47e3, y=47e3, z=47e3, c=500e3, s=47e3)
+RATE = dict(x=45e3, y=47e3, z=45e3, c=500e3, s=47e3)
 LAG = dict(x=1.8, y=1.8, z=1.8, c=1.0, s=8.0)
 GROUPS = 6 + (2 * 2 * WQ + 1 + NX) + 6 + len(EARLY) * (26 + 26 - 5) + len(LATE) * (26 - 2)
 

time: 96.3 us -> 95.6 us (level)
  no operation moved by 1% of the time
where the time goes in v6:
time: 95.6 us; the launch traced here: 95.5 us
  Pallas kernels  93.8 us (98%)
  local copies, waits for them, and re-layouts  1.62 us (2%)
    pallas_call x1, Pallas kernels, on_device(): pl.pallas_call(kernel, out_shape=jax.ShapeDtypeStruct((TOK, WIDTH), bf16)...  93.8 us

profile of v6, /device:TPU:2, one launch (start us, length us, event | category | flops | bytes accessed | tf_op | source)
XLA Modules:
  0.0 95.5 jit_solution(1262779505448105319)
XLA Ops:
  0.0 93.8 %block.1 = bf16[384,256]{1,0:T(8,128)(2,1)} custom-call(bf16[384,256]{1,0:T(8,128)(2,1)} %embeds.1, f32[1,8192]{1,0:T(1,128)} %bitcast.5, f32[1,8192]{1,0:T(1,128)} %bitcast.6, bf16[1024,768]{1,0:T(8,128)(2,1)} %w_qkv.1, bf16[4,2,128,256]{3,2,1,0:T(8,128)(2,1)} %bitcast.4, f32[1,256]{1,0:T(1,128)} %bitcast.7), custom_call_target="tpu_custom_call" | custom-call | tf_op jit(solution)/shard_map/block/pallas_call | solution.py:425
  93.8 1.6 %copy.8 = bf16[384,256]{1,0:T(8,128)(2,1)} copy(bf16[384,256]{1,0:T(8,128)(2,1)} %block.1) | data formatting | bytes 393216
